TPU v7x, 32 devices: a whole 2x2x4 slice. The times are simulated.
32 devices in a mesh: seq: 4 (over z), dp: 8 (over y, x, core).
Axes of the slice: x: 2, y: 2, z: 4, core: 2. Of those that a mesh axis runs over, the one named last changes fastest.
Arguments:
- stream: float32 [8, 512, 1152], P('dp', 'seq'), may hold values from -50 to 50
- stream_grad: float32 [8, 512, 1152], P('dp', 'seq'), may hold values from -6 to 6
- lengths: int32 [8, 4], P('dp'), may hold values from 1 to 384, 512 in all within a row
- w_qkv: bfloat16 [1152, 1536], P(('seq', 'dp')), may hold values from -0.1875 to 0.1875
- w_out: bfloat16 [1024, 1152], P(('seq', 'dp')), may hold values from -0.1875 to 0.1875
- w_gate: bfloat16 [6912, 1152], P(('seq', 'dp')), may hold values from -0.1875 to 0.1875
- w_up: bfloat16 [6912, 1152], P(('seq', 'dp')), may hold values from -0.1875 to 0.1875
- w_down: bfloat16 [6912, 1152], P(('seq', 'dp')), may hold values from -0.078125 to 0.078125
- g_attn_in: float32 [1152], replicated, may hold values from 0.25 to 1.75
- g_query: float32 [256], replicated, may hold values from 0.25 to 1.75
- g_key: float32 [256], replicated, may hold values from 0.25 to 1.75
- g_attn_out: float32 [1152], replicated, may hold values from 0.25 to 1.75
- g_ffn_in: float32 [1152], replicated, may hold values from 0.25 to 1.75
- g_ffn_out: float32 [1152], replicated, may hold values from 0.25 to 1.75
Outputs:
- result: float32 [8, 512, 1152], P('dp', 'seq')
- input_grad: float32 [8, 512, 1152], P('dp', 'seq')
- grad_w_qkv: float32 [1152, 1536], P(('seq', 'dp'))
- grad_w_out: float32 [1024, 1152], P(('seq', 'dp'))
- grad_w_gate: float32 [6912, 1152], P(('seq', 'dp'))
- grad_w_up: float32 [6912, 1152], P(('seq', 'dp'))
- grad_w_down: float32 [6912, 1152], P(('seq', 'dp'))
- grad_g_attn_in: float32 [1152], P(('seq', 'dp'))
- grad_g_query: float32 [256], P(('seq', 'dp'))
- grad_g_key: float32 [256], P(('seq', 'dp'))
- grad_g_attn_out: float32 [1152], P(('seq', 'dp'))
- grad_g_ffn_in: float32 [1152], P(('seq', 'dp'))
- grad_g_ffn_out: float32 [1152], P(('seq', 'dp'))
Inputs may be any that keep to these rules, and one draw needn't show every extreme that they name: Each row lists the lengths of the 4 sequences packed in order into one group; they sum to 512.
All inputs are finite; a program needn't handle non-finite values.
Results may differ from a plain program's by a relative error of at most 0.015.
Values may be sent and summed in bfloat16 or wider, within the bound.
A program may use at most 128 MiB of HBM per device.

v0:
```python
import math
import jax
import jax.numpy as jnp
from jax import lax
from jax.sharding import PartitionSpec as P

HEADS = 4
HEAD_DIM = 256
WINDOW = 512
EPSILON = 1e-06
GELU_SLOPE = math.sqrt(2.0 / math.pi)
GELU_CUBIC = 0.044715


def passed_along(value, axis, by):
    length = lax.axis_size(axis)
    pairs = [(i, i + by) for i in range(length) if 0 <= i + by < length]
    return lax.ppermute(value, axis, pairs)


def inv_root(vector):
    return lax.rsqrt(jnp.mean(vector * vector, axis=-1, keepdims=True) + EPSILON)


def norm_back(grad, unit_part, root_part, gain):
    scaled = grad * gain
    return root_part * (scaled - unit_part * jnp.mean(scaled * unit_part, axis=-1, keepdims=True))


def gelu_pair(gate):
    inner = jnp.tanh(GELU_SLOPE * (gate + GELU_CUBIC * gate * gate * gate))
    gelu_value = 0.5 * gate * (1.0 + inner)
    gelu_slope = 0.5 * (1.0 + inner) + 0.5 * gate * (1.0 - inner * inner) * GELU_SLOPE * (
        1.0 + 3.0 * GELU_CUBIC * gate * gate
    )
    return (gelu_value, gelu_slope)


def turn_half(vector):
    half = vector.shape[-1] // 2
    return jnp.concatenate([-vector[..., half:], vector[..., :half]], axis=-1)


def seq_begin(index, starts):
    return jnp.max(jnp.where(starts[None, :] <= index[:, None], starts[None, :], 0), axis=1)


def rope_tables(position, head):
    freq = jnp.exp(-math.log(10000.0) * jnp.arange(head // 2, dtype=jnp.float32) * (2.0 / head))
    angle = position[:, None] * freq[None, :]
    angle = jnp.concatenate([angle, angle], axis=1)
    return (jnp.cos(angle), jnp.sin(angle))


def dot32(left, right):
    return jnp.dot(left, right, preferred_element_type=jnp.float32)


def contract_rows(left, right):
    return lax.dot_general(
        left, right, (((0,), (0,)), ((), ())), preferred_element_type=jnp.float32
    )


def contract_cols(left, right):
    return lax.dot_general(
        left, right, (((1,), (1,)), ((), ())), preferred_element_type=jnp.float32
    )


def ffn_forward_fold(tokens_b, pieces):
    gate_rows, up_rows, down_rows = pieces
    gate_part = contract_cols(tokens_b, gate_rows)
    up_part = contract_cols(tokens_b, up_rows)
    gelu_value, gelu_slope = gelu_pair(gate_part)
    hidden = (gelu_value * up_part).astype(jnp.bfloat16)
    out_total = dot32(hidden, down_rows)
    return (out_total, gate_part, up_part)


def ffn_backward_fold(grad_b, gate_all, up_all, pieces):
    gate_rows, up_rows, down_rows = pieces
    hidden_grad = contract_cols(grad_b, down_rows)
    gelu_value, gelu_slope = gelu_pair(gate_all)
    dgate_b = (hidden_grad * up_all * gelu_slope).astype(jnp.bfloat16)
    dup_b = (hidden_grad * gelu_value).astype(jnp.bfloat16)
    in_total = dot32(dgate_b, gate_rows) + dot32(dup_b, up_rows)
    return (in_total, dgate_b, dup_b)


def ffn_weight_terms(tokens_b, grad_b, gate_all, up_all, dgate_all, dup_all):
    gelu_value, gelu_slope = gelu_pair(gate_all)
    hidden = (gelu_value * up_all).astype(jnp.bfloat16)
    return jnp.concatenate(
        [
            contract_rows(dgate_all, tokens_b),
            contract_rows(dup_all, tokens_b),
            contract_rows(hidden, grad_b),
        ],
        axis=1,
    )


def local(
    stream,
    stream_grad,
    lengths,
    w_qkv,
    w_out,
    w_gate,
    w_up,
    w_down,
    g_attn_in,
    g_query,
    g_key,
    g_attn_out,
    g_ffn_in,
    g_ffn_out,
):
    rows_in = stream[0]
    rows_grad = stream_grad[0]
    lens = lengths[0]
    rows = rows_in.shape[0]
    width = rows_in.shape[1]
    qwidth = HEADS * HEAD_DIM
    hops = (WINDOW + rows - 2) // rows
    keys = (hops + 1) * rows
    scale = 1.0 / math.sqrt(HEAD_DIM)
    qkv_full, out_full = (
        lax.all_gather(w_qkv, ("seq", "dp"), axis=0, tiled=True),
        lax.all_gather(w_out, ("seq", "dp"), axis=0, tiled=True),
    )
    block_id = lax.axis_index("seq")
    starts = jnp.cumsum(lens) - lens
    own_index = block_id * rows + jnp.arange(rows, dtype=jnp.int32)
    key_index = block_id * rows - hops * rows + jnp.arange(keys, dtype=jnp.int32)
    own_begin = seq_begin(own_index, starts)
    key_begin = seq_begin(key_index, starts)
    mask = (
        (key_index[None, :] >= 0)
        & (key_begin[None, :] == own_begin[:, None])
        & (key_index[None, :] <= own_index[:, None])
        & (own_index[:, None] - key_index[None, :] < WINDOW)
    )
    full_mask = mask[:, None, :]
    cos_t, sin_t = rope_tables((own_index - own_begin).astype(jnp.float32), HEAD_DIM)
    root_attn = inv_root(rows_in)
    unit_attn = rows_in * root_attn
    attn_input = (unit_attn * g_attn_in).astype(jnp.bfloat16)
    projected = dot32(attn_input, qkv_full)
    query = projected[:, :qwidth].reshape(rows, HEADS, HEAD_DIM)
    key_raw = projected[:, qwidth : qwidth + HEAD_DIM]
    value_raw = projected[:, qwidth + HEAD_DIM :]
    root_query = inv_root(query)
    unit_query = query * root_query
    query_norm = unit_query * g_query
    root_key = inv_root(key_raw)
    unit_key = key_raw * root_key
    key_norm = unit_key * g_key
    query_rot = query_norm * cos_t[:, None, :] + turn_half(query_norm) * sin_t[:, None, :]
    key_rot = key_norm * cos_t + turn_half(key_norm) * sin_t
    query_b = query_rot.astype(jnp.bfloat16)
    kv_own = jnp.concatenate([key_rot.astype(jnp.bfloat16), value_raw.astype(jnp.bfloat16)], axis=1)
    earlier = []
    for hop in range(hops, 0, -1):
        earlier.append(passed_along(kv_own, "seq", hop))
    kv_all = jnp.concatenate(earlier + [kv_own], axis=0)
    keys_b = kv_all[:, :HEAD_DIM]
    values_b = kv_all[:, HEAD_DIM:]
    scores = jnp.einsum("rhd,kd->rhk", query_b, keys_b, preferred_element_type=jnp.float32) * scale
    logsum = jnp.log(jnp.sum(jnp.where(full_mask, jnp.exp(scores), 0.0), axis=-1))
    probs = jnp.where(full_mask, jnp.exp(scores - logsum[..., None]), 0.0)
    probs_b = probs.astype(jnp.bfloat16)
    mixed = jnp.einsum("rhk,kd->rhd", probs_b, values_b, preferred_element_type=jnp.float32)
    mixed_b = mixed.reshape(rows, qwidth).astype(jnp.bfloat16)
    attn_out = dot32(mixed_b, out_full)
    root_post = inv_root(attn_out)
    unit_post = attn_out * root_post
    hidden_in = rows_in + unit_post * g_attn_out
    root_ffn = inv_root(hidden_in)
    unit_ffn = hidden_in * root_ffn
    ffn_input = (unit_ffn * g_ffn_in).astype(jnp.bfloat16)
    tokens_b = lax.all_gather(ffn_input, "seq", axis=0, tiled=True)
    out_part, gate_all, up_all = ffn_forward_fold(
        tokens_b,
        (
            lax.all_gather(w_gate, "dp", axis=0, tiled=True),
            lax.all_gather(w_up, "dp", axis=0, tiled=True),
            lax.all_gather(w_down, "dp", axis=0, tiled=True),
        ),
    )
    ffn_out = lax.psum_scatter(out_part, "seq", scatter_dimension=0, tiled=True)
    root_out = inv_root(ffn_out)
    unit_out = ffn_out * root_out
    result = hidden_in + unit_out * g_ffn_out
    grad_g_ffn_out = jnp.sum(rows_grad * unit_out, axis=0)
    ffn_grad_b = norm_back(rows_grad, unit_out, root_out, g_ffn_out).astype(jnp.bfloat16)
    grads_b = lax.all_gather(ffn_grad_b, "seq", axis=0, tiled=True)
    in_part, dgate_all, dup_all = ffn_backward_fold(
        grads_b,
        gate_all,
        up_all,
        (
            lax.all_gather(w_gate, "dp", axis=0, tiled=True),
            lax.all_gather(w_up, "dp", axis=0, tiled=True),
            lax.all_gather(w_down, "dp", axis=0, tiled=True),
        ),
    )
    ffn_in_grad = lax.psum_scatter(in_part, "seq", scatter_dimension=0, tiled=True)
    ffn_terms = lax.psum_scatter(
        ffn_weight_terms(tokens_b, grads_b, gate_all, up_all, dgate_all, dup_all).astype(
            jnp.bfloat16
        ),
        "dp",
        scatter_dimension=0,
        tiled=True,
    ).astype(jnp.float32)
    grad_w_gate = ffn_terms[:, :width]
    grad_w_up = ffn_terms[:, width : 2 * width]
    grad_w_down = ffn_terms[:, 2 * width :]
    grad_g_ffn_in = jnp.sum(ffn_in_grad * unit_ffn, axis=0)
    hidden_grad_in = rows_grad + norm_back(ffn_in_grad, unit_ffn, root_ffn, g_ffn_in)
    grad_g_attn_out = jnp.sum(hidden_grad_in * unit_post, axis=0)
    attn_grad_b = norm_back(hidden_grad_in, unit_post, root_post, g_attn_out).astype(jnp.bfloat16)
    mixed_grad_b = contract_cols(attn_grad_b, out_full).astype(jnp.bfloat16)
    mixed_grad3 = mixed_grad_b.reshape(rows, HEADS, HEAD_DIM)
    delta = jnp.sum(
        mixed_grad3.astype(jnp.float32)
        * mixed_b.reshape(rows, HEADS, HEAD_DIM).astype(jnp.float32),
        axis=-1,
    )
    scores_again = (
        jnp.einsum("rhd,kd->rhk", query_b, keys_b, preferred_element_type=jnp.float32) * scale
    )
    probs_again = jnp.where(full_mask, jnp.exp(scores_again - logsum[..., None]), 0.0)
    probs_again_b = probs_again.astype(jnp.bfloat16)
    value_grad_all = jnp.einsum(
        "rhk,rhd->kd", probs_again_b, mixed_grad3, preferred_element_type=jnp.float32
    )
    prob_grad = jnp.einsum("rhd,kd->rhk", mixed_grad3, values_b, preferred_element_type=jnp.float32)
    score_grad_b = (probs_again * (prob_grad - delta[..., None])).astype(jnp.bfloat16)
    query_rot_grad = (
        jnp.einsum("rhk,kd->rhd", score_grad_b, keys_b, preferred_element_type=jnp.float32) * scale
    )
    key_grad_all = (
        jnp.einsum("rhk,rhd->kd", score_grad_b, query_b, preferred_element_type=jnp.float32) * scale
    )
    kv_grad_all = jnp.concatenate([key_grad_all, value_grad_all], axis=1)
    kv_grad = kv_grad_all[hops * rows :]
    for hop in range(1, hops + 1):
        block = kv_grad_all[(hops - hop) * rows : (hops - hop + 1) * rows]
        kv_grad = kv_grad + passed_along(block.astype(jnp.bfloat16), "seq", -hop).astype(
            block.dtype
        )
    key_rot_grad = kv_grad[:, :HEAD_DIM]
    value_grad = kv_grad[:, HEAD_DIM:]
    query_norm_grad = query_rot_grad * cos_t[:, None, :] - turn_half(
        query_rot_grad * sin_t[:, None, :]
    )
    key_norm_grad = key_rot_grad * cos_t - turn_half(key_rot_grad * sin_t)
    grad_g_query = jnp.sum(query_norm_grad * unit_query, axis=(0, 1))
    grad_g_key = jnp.sum(key_norm_grad * unit_key, axis=0)
    query_grad = norm_back(query_norm_grad, unit_query, root_query, g_query)
    key_grad = norm_back(key_norm_grad, unit_key, root_key, g_key)
    qkv_grad_b = jnp.concatenate(
        [query_grad.reshape(rows, qwidth), key_grad, value_grad], axis=1
    ).astype(jnp.bfloat16)
    attn_in_grad = contract_cols(qkv_grad_b, qkv_full)
    grad_g_attn_in = jnp.sum(attn_in_grad * unit_attn, axis=0)
    input_grad = hidden_grad_in + norm_back(attn_in_grad, unit_attn, root_attn, g_attn_in)
    gain_terms = jnp.stack([grad_g_attn_in, grad_g_attn_out, grad_g_ffn_in, grad_g_ffn_out])
    head_terms = jnp.stack([grad_g_query, grad_g_key])
    out_term = contract_rows(mixed_b, attn_grad_b)
    qkv_term = contract_rows(attn_input, qkv_grad_b)
    owned_qkv, owned_out, owned_gains, owned_heads = (
        lax.psum_scatter(qkv_term, ("seq", "dp"), scatter_dimension=0, tiled=True),
        lax.psum_scatter(out_term, ("seq", "dp"), scatter_dimension=0, tiled=True),
        lax.psum_scatter(gain_terms, ("seq", "dp"), scatter_dimension=1, tiled=True),
        lax.psum_scatter(head_terms, ("seq", "dp"), scatter_dimension=1, tiled=True),
    )
    return (
        result[None],
        input_grad[None],
        owned_qkv,
        owned_out,
        grad_w_gate,
        grad_w_up,
        grad_w_down,
        owned_gains[0],
        owned_heads[0],
        owned_heads[1],
        owned_gains[1],
        owned_gains[2],
        owned_gains[3],
    )


def solution(mesh):
    return jax.shard_map(
        local,
        mesh=mesh,
        in_specs=(
            P("dp", "seq", None),
            P("dp", "seq", None),
            P("dp", None),
            P(("seq", "dp"), None),
            P(("seq", "dp"), None),
            P(("seq", "dp"), None),
            P(("seq", "dp"), None),
            P(("seq", "dp"), None),
            P(),
            P(),
            P(),
            P(),
            P(),
            P(),
        ),
        out_specs=(
            P("dp", "seq", None),
            P("dp", "seq", None),
            P(("seq", "dp"), None),
            P(("seq", "dp"), None),
            P(("seq", "dp"), None),
            P(("seq", "dp"), None),
            P(("seq", "dp"), None),
            P(("seq", "dp")),
            P(("seq", "dp")),
            P(("seq", "dp")),
            P(("seq", "dp")),
            P(("seq", "dp")),
            P(("seq", "dp")),
        ),
        check_vma=False,
    )
```

profile of v0, /device:TPU:0, one launch (start us, length us, event | category | flops | bytes accessed | tf_op | source)
XLA Modules:
  0.0 682.3 jit_solution(9453058917675593302)
XLA Ops:
  13.7 60.8 %all-gather.21.cloned.1.call-done = bf16[32,36,1536]{2,1,0:T(8,128)(2,1)} async-done(((bf16[1,36,1536]{2,1,0:T(8,128)(2,1)}), bf16[32,36,1536]{2,1,0:T(8,128)(2,1)}) %all-gather.21.cloned.1.call-update) | async-done | bytes 3538960 | tf_op jit(solution)/shard_map/all_gather | solution.py:130
  74.5 3.9 reshape.292
  78.4 1.8 fusion.48
  85.0 4.7 collective-permute-start.1
  89.7 1.9 collective-permute-start.2
  91.7 2.5 collective-permute-start.3
  95.1 2.1 reshape.288
  97.1 1.9 multiply_reduce_fusion.13
  107.1 1.4 convolution_multiply_fusion
  108.6 3.3 convolution_convert_fusion.4
  111.8 1.8 copy.84
  113.6 23.7 %all-gather.9.cloned.1.call-done = bf16[1024,1152]{1,0:T(8,128)(2,1)} async-done(((bf16[32,1152]{1,0:T(8,128)(2,1)}), bf16[1024,1152]{1,0:T(8,128)(2,1)}) %all-gather.9.cloned.1.call-update) | async-done | bytes 2359312 | tf_op jit(solution)/shard_map/all_gather | solution.py:131
  137.3 2.4 multiply_reduce_fusion.9
  143.9 29.8 %all-gather.13.cloned.1.call-done = bf16[1728,1152]{1,0:T(8,128)(2,1)} async-done(((bf16[216,1152]{1,0:T(8,128)(2,1)}), bf16[1728,1152]{1,0:T(8,128)(2,1)}) %all-gather.13.cloned.1.call-update) | async-done | bytes 3981328 | tf_op jit(solution)/shard_map/all_gather | solution.py:187
  173.7 32.3 %all-gather.11.cloned.1.call-done = bf16[512,1152]{1,0:T(8,128)(2,1)} async-done(((bf16[128,1152]{1,0:T(8,128)(2,1)}), bf16[512,1152]{1,0:T(8,128)(2,1)}) %all-gather.11.cloned.1.call-update) | async-done | bytes 1179664 | tf_op jit(solution)/shard_map/all_gather | solution.py:183
  206.0 6.8 fusion.51
  212.8 29.9 %all-gather.15.cloned.1.call-done = bf16[1728,1152]{1,0:T(8,128)(2,1)} async-done(((bf16[216,1152]{1,0:T(8,128)(2,1)}), bf16[1728,1152]{1,0:T(8,128)(2,1)}) %all-gather.15.cloned.1.call-update) | async-done | bytes 3981328 | tf_op jit(solution)/shard_map/all_gather | solution.py:188
  242.7 9.3 %multiply_convert_fusion.1 = (bf16[512,1728]{0,1:T(8,128)(2,1)}, f32[512,1728]{0,1:T(8,128)}) fusion(f32[512,1728]{0,1:T(8,128)} %fusion.51, bf16[512,1152]{1,0:T(8,128)(2,1)} %all-gather.11.cloned.1.call-done, bf16[1728,1152]{1,0:T(8,128)(2,1)} %all-gather.15.cloned.1.call-done), kind=kOutput, calls=%fused_computation.15 | convolution fusion | flops 2047279104 | bytes 14008320 | tf_op jit(solution)/shard_map/dot_general | solution.py:66
  252.0 28.2 %all-gather.17.cloned.1.call-done = bf16[1728,1152]{1,0:T(8,128)(2,1)} async-done(((bf16[216,1152]{1,0:T(8,128)(2,1)}), bf16[1728,1152]{1,0:T(8,128)(2,1)}) %all-gather.17.cloned.1.call-update) | async-done | bytes 3981328 | tf_op jit(solution)/shard_map/all_gather | solution.py:189
  280.2 6.7 fusion.52
  286.9 47.8 %reduce-scatter.11.cloned.1.call-done = f32[128,1152]{1,0:T(8,128)} async-done(((f32[512,1152]{1,0:T(8,128)}), f32[128,1152]{1,0:T(8,128)}) %reduce-scatter.11.cloned.1.call-update) | async-done | bytes 589840 | tf_op jit(solution)/shard_map/reduce_scatter | solution.py:192
  335.9 2.1 fusion.20
  338.0 2.5 multiply_convert_fusion.3
  341.2 29.2 %all-gather.19.cloned.1.call-done = bf16[512,1152]{1,0:T(8,128)(2,1)} async-done(((bf16[128,1152]{1,0:T(8,128)(2,1)}), bf16[512,1152]{1,0:T(8,128)(2,1)}) %all-gather.19.cloned.1.call-update) | async-done | bytes 1179664 | tf_op jit(solution)/shard_map/all_gather | solution.py:198
  370.4 9.5 %multiply_convert_fusion = (bf16[512,1728]{0,1:T(8,128)(2,1)S(1)}, bf16[512,1728]{0,1:T(8,128)(2,1)S(1)}) fusion(f32[512,1728]{0,1:T(8,128)} %fusion.51, f32[512,1728]{0,1:T(8,128)} %get-tuple-element.66, bf16[512,1152]{1,0:T(8,128)(2,1)} %all-gather.19.cloned.1.call-done, bf16[1728,1152]{1,0:T(8,128)(2,1)} %all-gather.17.cloned.1.call-done), kind=kOutput, calls=%fused_computation.14 | convolution fusion | flops 2058780672 | bytes 15777792 | tf_op jit(solution)/shard_map/dot_general | solution.py:66
  379.9 2.7 fusion.53
  383.3 4.1 convolution_add_fusion
  387.7 4.4 convolution_convert_fusion
  392.1 2.5 convolution_convert_fusion.1
  394.6 2.5 convolution_convert_fusion.2
  397.0 5.0 pad_maximum_fusion
  402.1 3.5 fusion.13
  406.2 28.3 %reduce-scatter.13.cloned.1.call-done = f32[128,1152]{1,0:T(8,128)} async-done(((f32[512,1152]{1,0:T(8,128)}), f32[128,1152]{1,0:T(8,128)}) %reduce-scatter.13.cloned.1.call-update) | async-done | bytes 589840 | tf_op jit(solution)/shard_map/reduce_scatter | solution.py:209
  434.5 2.2 multiply_reduce_fusion
  436.7 2.8 multiply_reduce_fusion.1
  441.2 1.6 convolution_convert_fusion.3
  442.8 1.8 copy.85
  444.6 1.8 copy.87
  447.8 4.0 convolution_bitcast_fusion
  451.8 2.5 fusion.14
  461.1 1.5 collective-permute-start.4
  462.7 3.1 fusion.54
  468.7 4.8 collective-permute-done.5
  474.8 1.4 broadcast_multiply_fusion.2
  476.3 1.8 multiply_reduce_fusion.14
  478.5 1.6 multiply_convert_fusion.7
  480.1 1.5 multiply_reduce_fusion.10
  482.9 1.6 copy.93
  484.5 1.6 copy.92
  486.0 2.1 multiply_convert_fusion.6
  488.2 1.8 copy.88
  489.9 5.3 fusion.34
  495.2 103.8 %fusion = f32[40,1536]{1,0:T(8,128)} fusion(f32[1152,1536]{1,0:T(8,128)} %fusion.34), kind=kCustom, calls=%all-reduce-scatter | all-reduce-scatter fusion | flops 1966081 | bytes 7323648
  599.1 1.4 slice.146
  600.5 3.1 collective-permute-start.10
  603.6 7.6 %collective-permute-start.9 = (f32[40,1536]{1,0:T(8,128)}, f32[40,1536]{1,0:T(8,128)}, u32[]{:S(2)}, u32[]{:S(2)}) collective-permute-start(f32[40,1536]{1,0:T(8,128)} %fusion), channel_id=1, source_target_pairs={{0,2},{1,3},{2,4},{3,5},{4,6},{5,7},{6,8},{7,9},{8,10},{9,11},{10,... | collective-permute-start | bytes 737288
  611.2 3.0 collective-permute-start.8
  614.2 2.3 collective-permute-start.11
  616.5 3.3 multiply_reduce_fusion.2
  619.9 39.2 %all-reduce.5 = (f32[4,1152]{1,0:T(4,128)S(1)}, f32[2,256]{1,0:T(2,128)S(1)}) all-reduce(f32[4,1152]{1,0:T(4,128)S(1)} %pad_maximum_fusion.7, f32[2,256]{1,0:T(2,128)S(1)} %pad_maximum_fusion.8), channel_id=7, replica_groups=mesh['seq'=4,'dp'=8] {'seq','dp'}, use_global_device_ids=true, to_apply=%region_26.27.clone | all-reduce | flops 5120 | bytes 40960
  659.8 2.4 add_bitcast_fusion
  662.8 4.1 concatenate.50
  667.6 3.0 fusion.49
  670.7 4.9 reduce-scatter.15.cloned.1.call-done
  (217 shorter events, 45.4 us)
Async XLA Ops:
  7.2 67.3 %all-gather.21.cloned.1.call-start = ((), (), s32[]{:S(2)}) async-start(), calls=%async_computation.13 | async-start | bytes 4055040 | tf_op jit(solution)/shard_map/all_gather | solution.py:130
  7.9 129.4 %all-gather.9.cloned.1.call-start = ((), (), s32[]{:S(2)}) async-start(), calls=%async_computation.4 | async-start | bytes 2433024 | tf_op jit(solution)/shard_map/all_gather | solution.py:131
  8.7 165.1 %all-gather.13.cloned.1.call-start = ((), (), s32[]{:S(2)}) async-start(), calls=%async_computation.6 | async-start | bytes 4478976 | tf_op jit(solution)/shard_map/all_gather | solution.py:187
  9.4 196.6 %all-gather.11.cloned.1.call-start = ((), (), s32[]{:S(2)}) async-start(), calls=%async_computation.5 | async-start | bytes 1474560 | tf_op jit(solution)/shard_map/all_gather | solution.py:183
  12.4 66.0 %copy-start.44 = (f32[128]{0:T(128)}, f32[128]{0:T(128)S(1)}, u32[]{:S(2)}) copy-start(f32[128]{0:T(128)S(1)} %add_rsqrt_fusion.5) | copy-start | bytes 1540
  13.7 64.7 %copy-start.30 = (f32[1152]{0:T(1024)S(1)}, f32[1152]{0:T(1024)}, u32[]{:S(2)}) copy-start(f32[1152]{0:T(1024)} %param.22) | copy-start | bytes 13828
  80.2 13.9 %copy-start.14 = (f32[128,1536]{1,0:T(8,128)}, f32[128,1536]{1,0:T(8,128)S(1)}, u32[]{:S(2)}) copy-start(f32[128,1536]{1,0:T(8,128)S(1)} %fusion.48) | copy-start | bytes 2359300
  80.2 19.7 %copy-start.42 = (f32[256]{0:T(256)S(1)}, f32[256]{0:T(256)}, u32[]{:S(2)}) copy-start(f32[256]{0:T(256)} %param.23) | copy-start | bytes 3076
  80.3 3.4 copy-start.28
  80.4 4.6 copy-start.46
  83.7 18.7 %collective-permute-start = (bf16[128,512]{1,0:T(8,128)(2,1)}, bf16[128,512]{1,0:T(8,128)(2,1)}, u32[]{:S(2)}, u32[]{:S(2)}) collective-permute-start(bf16[128,512]{1,0:T(8,128)(2,1)} %pad_maximum_fusion.6), channel_id=1, source_target_pairs={} | collective-permute-start | bytes 393224 | tf_op jit(solution)/shard_map/ppermute | solution.py:18
  85.0 18.4 %collective-permute-start.1 = (bf16[128,512]{1,0:T(8,128)(2,1)}, bf16[128,512]{1,0:T(8,128)(2,1)}, u32[]{:S(2)}, u32[]{:S(2)}) collective-permute-start(bf16[128,512]{1,0:T(8,128)(2,1)} %pad_maximum_fusion.6), channel_id=1, source_target_pairs={{0,24},{1,25},{2,26},{3,27},{4,28},{5,29},{6,30},{7,31}} | collective-permute-start | bytes 393224 | tf_op jit(solution)/shard_map/ppermute | solution.py:18
  89.7 14.6 %collective-permute-start.2 = (bf16[128,512]{1,0:T(8,128)(2,1)}, bf16[128,512]{1,0:T(8,128)(2,1)}, u32[]{:S(2)}, u32[]{:S(2)}) collective-permute-start(bf16[128,512]{1,0:T(8,128)(2,1)} %pad_maximum_fusion.6), channel_id=1, source_target_pairs={{0,16},{8,24},{1,17},{9,25},{2,18},{10,26},{3,19},{11,27},{4,20},{... | collective-permute-start | bytes 393224 | tf_op jit(solution)/shard_map/ppermute | solution.py:18
  91.7 13.6 %collective-permute-start.3 = (bf16[128,512]{1,0:T(8,128)(2,1)}, bf16[128,512]{1,0:T(8,128)(2,1)}, u32[]{:S(2)}, u32[]{:S(2)}) collective-permute-start(bf16[128,512]{1,0:T(8,128)(2,1)} %pad_maximum_fusion.6), channel_id=1, source_target_pairs={{0,8},{8,16},{16,24},{1,9},{9,17},{17,25},{2,10},{10,18},{18,26},{... | collective-permute-start | bytes 393224 | tf_op jit(solution)/shard_map/ppermute | solution.py:18
  99.9 6.3 copy-start.33
  99.9 6.3 copy-start.27
  100.0 6.3 copy-start.29
  102.4 3.9 copy-start.19
  137.3 4.3 copy-start.31
  142.4 100.3 %all-gather.15.cloned.1.call-start = ((), (), s32[]{:S(2)}) async-start(), calls=%async_computation.7 | async-start | bytes 4478976 | tf_op jit(solution)/shard_map/all_gather | solution.py:188
  143.0 137.1 %all-gather.17.cloned.1.call-start = ((), (), s32[]{:S(2)}) async-start(), calls=%async_computation.8 | async-start | bytes 4478976 | tf_op jit(solution)/shard_map/all_gather | solution.py:189
  143.6 191.1 %reduce-scatter.11.cloned.1.call-start = ((), (), s32[]{:S(2)}) async-start(), calls=%async_computation.9 | async-start | bytes 2949120 | tf_op jit(solution)/shard_map/reduce_scatter | solution.py:192
  286.9 83.5 %all-gather.19.cloned.1.call-start = ((), (), s32[]{:S(2)}) async-start(), calls=%async_computation.10 | async-start | bytes 1474560 | tf_op jit(solution)/shard_map/all_gather | solution.py:198
  340.6 93.9 %reduce-scatter.13.cloned.1.call-start = ((), (), s32[]{:S(2)}) async-start(), calls=%async_computation.11 | async-start | bytes 2949120 | tf_op jit(solution)/shard_map/reduce_scatter | solution.py:209
  370.4 9.5 %copy-start.54 = (bf16[1728,1152]{1,0:T(8,128)(2,1)S(1)}, bf16[1728,1152]{1,0:T(8,128)(2,1)}, u32[]{:S(2)}) copy-start(bf16[1728,1152]{1,0:T(8,128)(2,1)} %all-gather.13.cloned.1.call-done) | copy-start | bytes 11943940
  379.9 2.7 copy-start.56
  379.9 3.4 copy-start.4
  387.4 280.2 %reduce-scatter.17.cloned.1.call-start = ((), (), s32[]{:S(2)}) async-start(), calls=%async_computation.14 | async-start | bytes 13436928
  387.6 4.4 copy-start.12
  387.7 4.4 copy-start.55
  402.0 273.5 %reduce-scatter.15.cloned.1.call-start = ((), (), s32[]{:S(2)}) async-start(), calls=%async_computation.12 | async-start | bytes 4866048 | tf_op jit(solution)/shard_map/reduce_scatter | solution.py:277
  402.1 3.5 copy-start.35
  434.5 5.8 copy-start.6
  434.5 5.8 copy-start.32
  434.5 5.8 copy-start.49
  436.7 4.5 copy-start.7
  451.8 3.3 copy-start.20
  451.8 4.6 copy-start.17
  455.1 7.5 %copy-start.16 = (bf16[128,1152]{1,0:T(8,128)(2,1)S(1)}, bf16[128,1152]{1,0:T(8,128)(2,1)}, u32[]{:S(2)}) copy-start(bf16[128,1152]{1,0:T(8,128)(2,1)} %copy-done.15) | copy-start | bytes 884740
  455.1 7.5 %copy-start.18 = (bf16[128,4,256]{0,2,1:T(8,128)(2,1)S(1)}, bf16[128,4,256]{0,2,1:T(8,128)(2,1)}, u32[]{:S(2)}) copy-start(bf16[128,4,256]{0,2,1:T(8,128)(2,1)} %copy.84) | copy-start | bytes 786436
  457.2 10.5 %collective-permute-start.7 = (bf16[128,512]{1,0:T(8,128)(2,1)}, bf16[128,512]{1,0:T(8,128)(2,1)}, u32[]{:S(2)}, u32[]{:S(2)}) collective-permute-start(bf16[128,512]{1,0:T(8,128)(2,1)} %get-tuple-element.38), channel_id=1, source_target_pairs={} | collective-permute-start | bytes 393224 | tf_op jit(solution)/shard_map/ppermute | solution.py:18
  458.5 10.2 %collective-permute-start.6 = (bf16[128,512]{1,0:T(8,128)(2,1)}, bf16[128,512]{1,0:T(8,128)(2,1)}, u32[]{:S(2)}, u32[]{:S(2)}) collective-permute-start(bf16[128,512]{1,0:T(8,128)(2,1)} %get-tuple-element.39), channel_id=1, source_target_pairs={{24,0},{25,1},{26,2},{27,3},{28,4},{29,5},{30,6},{31,7}} | collective-permute-start | bytes 393224 | tf_op jit(solution)/shard_map/ppermute | solution.py:18
  459.8 13.7 %collective-permute-start.5 = (bf16[128,512]{1,0:T(8,128)(2,1)}, bf16[128,512]{1,0:T(8,128)(2,1)}, u32[]{:S(2)}, u32[]{:S(2)}) collective-permute-start(bf16[128,512]{1,0:T(8,128)(2,1)} %get-tuple-element.40), channel_id=1, source_target_pairs={{16,0},{24,8},{17,1},{25,9},{18,2},{26,10},{19,3},{27,11},{20,4},{... | collective-permute-start | bytes 393224 | tf_op jit(solution)/shard_map/ppermute | solution.py:18
  461.1 4.6 copy-start.36
  461.1 12.3 %collective-permute-start.4 = (bf16[128,512]{1,0:T(8,128)(2,1)}, bf16[128,512]{1,0:T(8,128)(2,1)}, u32[]{:S(2)}, u32[]{:S(2)}) collective-permute-start(bf16[128,512]{1,0:T(8,128)(2,1)} %get-tuple-element.37), channel_id=1, source_target_pairs={{8,0},{16,8},{24,16},{9,1},{17,9},{25,17},{10,2},{18,10},{26,18},{... | collective-permute-start | bytes 393224 | tf_op jit(solution)/shard_map/ppermute | solution.py:18
  467.7 8.6 %copy-start.25 = (f32[128,128]{1,0:T(8,128)S(1)}, f32[128,128]{1,0:T(8,128)}, u32[]{:S(2)}) copy-start(f32[128,128]{1,0:T(8,128)} %copy-done.24) | copy-start | bytes 196612
  467.7 8.6 %copy-start.41 = (f32[256]{0:T(256)S(1)}, f32[256]{0:T(256)}, u32[]{:S(2)}) copy-start(f32[256]{0:T(256)} %param.24) | copy-start | bytes 3076
  467.7 8.6 %copy-start.47 = (f32[128]{0:T(128)S(1)}, f32[128]{0:T(128)}, u32[]{:S(2)}) copy-start(f32[128]{0:T(128)} %copy-done.46) | copy-start | bytes 1540
  467.7 10.3 %copy-start.9 = (bf16[128,4,640]{2,0,1:T(8,128)(2,1)S(1)}, bf16[128,4,640]{2,0,1:T(8,128)(2,1)}, u32[]{:S(2)}) copy-start(bf16[128,4,640]{2,0,1:T(8,128)(2,1)} %copy-done.8) | copy-start | bytes 1966084
  467.7 10.3 %copy-start.22 = (bf16[640,512]{1,0:T(8,128)(2,1)S(1)}, bf16[640,512]{1,0:T(8,128)(2,1)}, u32[]{:S(2)}) copy-start(bf16[640,512]{1,0:T(8,128)(2,1)} %copy-done.21) | copy-start | bytes 1966084
  474.8 5.3 copy-start.2
  474.8 5.3 copy-start.34
  474.8 5.3 copy-start.43
  495.2 121.3 %copy-start.45 = (f32[128]{0:T(128)S(1)}, f32[128]{0:T(128)}, u32[]{:S(2)}) copy-start(f32[128]{0:T(128)} %copy-done.44) | copy-start | bytes 1540
  600.5 19.4 %copy-start.51 = (f32[256]{0:T(256)S(1)}, f32[256]{0:T(256)}, u32[]{:S(2)}) copy-start(f32[256]{0:T(256)} %get-tuple-element.21) | copy-start | bytes 3076
  600.5 19.4 %copy-start.52 = (f32[256]{0:T(256)S(1)}, f32[256]{0:T(256)}, u32[]{:S(2)}) copy-start(f32[256]{0:T(256)} %get-tuple-element.23) | copy-start | bytes 3076
  600.5 19.4 %copy-start.37 = (f32[1,1152]{1,0:T(1,128)S(1)}, f32[1,1152]{1,0:T(1,128)}, u32[]{:S(2)}) copy-start(f32[1,1152]{1,0:T(1,128)} %stack.27) | copy-start | bytes 13828
  600.5 19.4 %copy-start.38 = (f32[1,1152]{1,0:T(1,128)S(1)}, f32[1,1152]{1,0:T(1,128)}, u32[]{:S(2)}) copy-start(f32[1,1152]{1,0:T(1,128)} %stack.26) | copy-start | bytes 13828
  600.5 19.4 %copy-start.39 = (f32[1,1152]{1,0:T(1,128)S(1)}, f32[1,1152]{1,0:T(1,128)}, u32[]{:S(2)}) copy-start(f32[1,1152]{1,0:T(1,128)} %stack.25) | copy-start | bytes 13828
  600.5 62.3 %collective-permute-start.10 = (f32[40,1536]{1,0:T(8,128)}, f32[40,1536]{1,0:T(8,128)}, u32[]{:S(2)}, u32[]{:S(2)}) collective-permute-start(f32[40,1536]{1,0:T(8,128)} %fusion), channel_id=1, source_target_pairs={{0,3},{1,4},{2,5},{3,6},{4,7},{5,8},{6,9},{7,10},{8,11},{9,12},{10... | collective-permute-start | bytes 737288
  603.6 59.2 %collective-permute-start.9 = (f32[40,1536]{1,0:T(8,128)}, f32[40,1536]{1,0:T(8,128)}, u32[]{:S(2)}, u32[]{:S(2)}) collective-permute-start(f32[40,1536]{1,0:T(8,128)} %fusion), channel_id=1, source_target_pairs={{0,2},{1,3},{2,4},{3,5},{4,6},{5,7},{6,8},{7,9},{8,10},{9,11},{10,... | collective-permute-start | bytes 737288
  611.2 51.6 %collective-permute-start.8 = (f32[40,1536]{1,0:T(8,128)}, f32[40,1536]{1,0:T(8,128)}, u32[]{:S(2)}, u32[]{:S(2)}) collective-permute-start(f32[40,1536]{1,0:T(8,128)} %fusion), channel_id=1, source_target_pairs={{0,1},{1,2},{2,3},{3,4},{4,5},{5,6},{6,7},{7,8},{8,9},{9,10},{10,1... | collective-permute-start | bytes 737288
  614.2 48.6 %collective-permute-start.11 = (f32[4,1536]{1,0:T(4,128)}, f32[4,1536]{1,0:T(4,128)}, u32[]{:S(2)}, u32[]{:S(2)}) collective-permute-start(f32[4,1536]{1,0:T(4,128)} %slice.146), channel_id=1, source_target_pairs={{0,4},{1,5},{2,6},{3,7},{4,8},{5,9},{6,10},{7,11},{8,12},{9,13},{1... | collective-permute-start | bytes 73736
  619.8 43.0 %copy-start.23 = (f32[40,1536]{1,0:T(8,128)S(1)}, f32[40,1536]{1,0:T(8,128)}, u32[]{:S(2)}) copy-start(f32[40,1536]{1,0:T(8,128)} %fusion) | copy-start | bytes 737284
  (17 other events, 22.1 us)
Sparse Core Ops, SparseCore 0:
  10.9 63.5 all-gather.20
  77.4 59.8 all-gather.8
  139.2 34.4 all-gather.12
  175.7 30.2 all-gather.10
  207.8 34.9 all-gather.14
  244.5 35.6 all-gather.16
  287.0 47.6 reduce-scatter.10
  340.7 29.6 all-gather.18
  387.5 46.9 reduce-scatter.12
  437.9 104.7 reduce-scatter.16
  548.7 126.7 reduce-scatter.14
where the time goes:
time: 689 us; the launch traced here: 682 us
  waiting for transfers between devices  324 us (47%)
  blocking collectives  143 us (21%)
  matrix products  77.7 us (11%)
  other arithmetic  46.2 us (7%)
  local copies, waits for them, and re-layouts  43.2 us (6%)
  starting transfers between devices  33.3 us (5%)
  between operations  15 us (2%)
    unnamed x2, blocking collectives  143 us
    all_gather x1, waiting for transfers between devices, local(): lax.all_gather(w_qkv, ('seq', 'dp'), axis=0, tiled=True)  60.8 us
    reduce_scatter x1, waiting for transfers between devices, local(): ffn_out = lax.psum_scatter(out_part, 'seq', scatter_dimension=0, tiled=True)  47.8 us
    all_gather x1, waiting for transfers between devices, local(): tokens_b = lax.all_gather(ffn_input, 'seq', axis=0, tiled=True)  32.3 us
    dot_general x5, matrix products, contract_cols(): lax.dot_general(left, right, (((1,), (1,)), ((), ())), preferred_element_...  30.4 us
    all_gather x1, waiting for transfers between devices, local(): lax.all_gather(w_up, 'dp', axis=0, tiled=True)  29.9 us
    all_gather x1, waiting for transfers between devices, local(): lax.all_gather(w_gate, 'dp', axis=0, tiled=True)  29.8 us
    all_gather x1, waiting for transfers between devices, local(): grads_b = lax.all_gather(ffn_grad_b, 'seq', axis=0, tiled=True)  29.2 us
  transfers between devices with their start and end apart: 23, of which 12 were waited for; matrix products, arithmetic and copies ran while one was open for 34% of the time, Pallas kernels for 0%

commit v1 on v0

--- a/solution.py
+++ b/solution.py
@@ -3,6 +3,7 @@
 import jax.numpy as jnp
 from jax import lax
 from jax.sharding import PartitionSpec as P
+from jax.lax import axis_index, axis_size, ppermute
 
 HEADS = 4
 HEAD_DIM = 256
@@ -10,6 +11,30 @@
 EPSILON = 1e-06
 GELU_SLOPE = math.sqrt(2.0 / math.pi)
 GELU_CUBIC = 0.044715
+
+
+def update_frames(s0, d_out):
+    long_array = list(s0.shape[1:])
+    long_array[d_out] *= s0.shape[0]
+    return jnp.moveaxis(s0, 0, d_out).reshape(long_array)
+
+
+def drive_frames(my_tile, axis_key):
+    after = axis_size(axis_key)
+    taken_in = axis_index(axis_key)
+    h_now, f_next = (after, taken_in)
+    passed, outcome_arr = (my_tile[None], 1)
+    while outcome_arr < h_now:
+        e_now = range(h_now)
+        item_now = map(lambda num: (num, num ^ outcome_arr), e_now)
+        x_new = list(item_now)
+        mat_out = ppermute(passed, axis_key, perm=x_new)
+        built = f_next & outcome_arr == 0
+        y2 = jnp.where(built, passed, mat_out)
+        arr_now = jnp.where(built, mat_out, passed)
+        passed = jnp.concatenate([y2, arr_now])
+        outcome_arr *= 2
+    return passed
 
 
 def passed_along(value, axis, by):
@@ -126,8 +151,13 @@
     hops = (WINDOW + rows - 2) // rows
     keys = (hops + 1) * rows
     scale = 1.0 / math.sqrt(HEAD_DIM)
+
+    def compute_stops_all(arr_in, original, array_dim):
+        back = drive_frames(arr_in, original)
+        return update_frames(back, array_dim)
+
     qkv_full, out_full = (
-        lax.all_gather(w_qkv, ("seq", "dp"), axis=0, tiled=True),
+        compute_stops_all(w_qkv, ("seq", "dp"), 0),
         lax.all_gather(w_out, ("seq", "dp"), axis=0, tiled=True),
     )
     block_id = lax.axis_index("seq")

time: 689 us -> 743 us (1.078)
  waiting for transfers between devices: 324 us -> 355 us
  starting transfers between devices: 33.3 us -> 42.1 us
    ppermute x0 -> x5, waiting for transfers between devices: none -> 115 us  [drive_frames(): mat_out = ppermute(passed, axis_key, perm=x_new)]
    all_gather x1 -> x0, waiting for transfers between devices: 60.8 us -> none  [local(): lax.all_gather(w_qkv, ('seq', 'dp'), axis=0, tiled=True)]
    all_gather x1, waiting for transfers between devices: 23.7 us -> 0.01 us  [local(): lax.all_gather(w_out, ('seq', 'dp'), axis=0, tiled=True)]
    ppermute x0 -> x5, starting transfers between devices: none -> 9.18 us  [drive_frames(): mat_out = ppermute(passed, axis_key, perm=x_new)]
    unnamed x126 -> x129, local copies, waits for them, and re-layouts: 21 us -> 17.2 us
  transfers between devices with their start and end apart: 23 -> 27, of which waited for: 12 -> 15; matrix products, arithmetic and copies ran while one was open for 34% -> 32% of each run, Pallas kernels for 0% -> 0%
where the time goes in v1:
time: 743 us; the launch traced here: 733 us
  waiting for transfers between devices  355 us (48%)
  blocking collectives  144 us (19%)
  matrix products  77.1 us (10%)
  other arithmetic  53 us (7%)
  local copies, waits for them, and re-layouts  45.4 us (6%)
  starting transfers between devices  42.1 us (6%)
  between operations  15.7 us (2%)
    unnamed x2, blocking collectives  144 us
    ppermute x5, waiting for transfers between devices, drive_frames(): mat_out = ppermute(passed, axis_key, perm=x_new)  115 us
    reduce_scatter x1, waiting for transfers between devices, local(): ffn_out = lax.psum_scatter(out_part, 'seq', scatter_dimension=0, tiled=True)  47.8 us
    all_gather x1, waiting for transfers between devices, local(): lax.all_gather(w_gate, 'dp', axis=0, tiled=True)  36.8 us
    all_gather x1, waiting for transfers between devices, local(): lax.all_gather(w_up, 'dp', axis=0, tiled=True)  30.7 us
    dot_general x5, matrix products, contract_cols(): lax.dot_general(left, right, (((1,), (1,)), ((), ())), preferred_element_...  30.4 us
    all_gather x1, waiting for transfers between devices, local(): grads_b = lax.all_gather(ffn_grad_b, 'seq', axis=0, tiled=True)  29.5 us
    reduce_scatter x1, waiting for transfers between devices, local(): lax.psum_scatter(in_part, 'seq', scatter_dimension=0, tiled=True)  28.2 us
  transfers between devices with their start and end apart: 27, of which 15 were waited for; matrix products, arithmetic and copies ran while one was open for 32% of the time, Pallas kernels for 0%

profile of v1, /device:TPU:0, one launch (start us, length us, event | category | flops | bytes accessed | tf_op | source)
XLA Modules:
  0.0 733.0 jit_solution(9301193430338061364)
XLA Ops:
  9.9 2.9 collective-permute-start.1
  12.8 6.3 collective-permute-done.1
  19.2 1.8 collective-permute-start.2
  21.0 10.9 %collective-permute-done.2 = bf16[4,36,1536]{2,1,0:T(8,128)(2,1)S(1)} collective-permute-done((bf16[4,36,1536]{2,1,0:T(8,128)(2,1)S(1)}, bf16[4,36,1536]{2,1,0:T(8,128)(2,1)S(1)}, u32[]{:S(2)}, u32[]{:S(2)}) %collective-permute-start.2) | collective-permute-done | bytes 442400 | tf_op jit(solution)/shard_map/ppermute | solution.py:31
  34.0 18.8 %collective-permute-done.3 = bf16[8,36,1536]{2,0,1:T(8,128)(2,1)} collective-permute-done((bf16[8,36,1536]{2,0,1:T(8,128)(2,1)S(1)}, bf16[8,36,1536]{2,0,1:T(8,128)(2,1)}, u32[]{:S(2)}, u32[]{:S(2)}) %collective-permute-start.3) | collective-permute-done | bytes 884768 | tf_op jit(solution)/shard_map/ppermute | solution.py:31
  52.9 1.8 broadcast_select_fusion.3
  54.9 1.7 copy.117
  56.6 2.3 collective-permute-start.4
  60.9 78.0 %collective-permute-done.4 = bf16[16,36,1536]{2,0,1:T(8,128)(2,1)} collective-permute-done((bf16[16,36,1536]{2,0,1:T(8,128)(2,1)}, bf16[16,36,1536]{2,0,1:T(8,128)(2,1)}, u32[]{:S(2)}, u32[]{:S(2)}) %collective-permute-start.4) | collective-permute-done | bytes 1769504 | tf_op jit(solution)/shard_map/ppermute | solution.py:31
  138.9 3.6 broadcast_select_fusion.1
  142.5 2.3 pad_maximum_fusion.1
  144.8 4.0 reshape.305
  148.8 1.8 fusion.29
  155.4 5.3 collective-permute-start.6
  160.7 1.9 collective-permute-start.7
  162.7 2.5 collective-permute-start.8
  166.0 2.1 reshape.306
  168.1 1.9 multiply_reduce_fusion.13
  179.5 3.2 convolution_convert_fusion.4
  182.7 1.8 copy.122
  184.5 2.4 multiply_reduce_fusion.9
  191.8 26.5 %all-gather.9.cloned.1.call-done = bf16[512,1152]{1,0:T(8,128)(2,1)} async-done(((bf16[128,1152]{1,0:T(8,128)(2,1)}), bf16[512,1152]{1,0:T(8,128)(2,1)}) %all-gather.9.cloned.1.call-update) | async-done | bytes 1179664 | tf_op jit(solution)/shard_map/all_gather | solution.py:213
  218.3 36.8 %all-gather.11.cloned.1.call-done = bf16[1728,1152]{1,0:T(8,128)(2,1)} async-done(((bf16[216,1152]{1,0:T(8,128)(2,1)}), bf16[1728,1152]{1,0:T(8,128)(2,1)}) %all-gather.11.cloned.1.call-update) | async-done | bytes 3981328 | tf_op jit(solution)/shard_map/all_gather | solution.py:217
  255.2 6.7 fusion.57
  261.9 30.7 %all-gather.13.cloned.1.call-done = bf16[1728,1152]{1,0:T(8,128)(2,1)} async-done(((bf16[216,1152]{1,0:T(8,128)(2,1)}), bf16[1728,1152]{1,0:T(8,128)(2,1)}) %all-gather.13.cloned.1.call-update) | async-done | bytes 3981328 | tf_op jit(solution)/shard_map/all_gather | solution.py:218
  292.6 9.3 %multiply_convert_fusion.1 = (bf16[512,1728]{0,1:T(8,128)(2,1)}, f32[512,1728]{0,1:T(8,128)}) fusion(f32[512,1728]{0,1:T(8,128)} %fusion.57, bf16[512,1152]{1,0:T(8,128)(2,1)} %all-gather.9.cloned.1.call-done, bf16[1728,1152]{1,0:T(8,128)(2,1)} %all-gather.13.cloned.1.call-done), kind=kOutput, calls=%fused_computation.16 | convolution fusion | flops 2047279104 | bytes 14008320 | tf_op jit(solution)/shard_map/dot_general | solution.py:91
  301.9 28.2 %all-gather.15.cloned.1.call-done = bf16[1728,1152]{1,0:T(8,128)(2,1)} async-done(((bf16[216,1152]{1,0:T(8,128)(2,1)}), bf16[1728,1152]{1,0:T(8,128)(2,1)}) %all-gather.15.cloned.1.call-update) | async-done | bytes 3981328 | tf_op jit(solution)/shard_map/all_gather | solution.py:219
  330.1 6.7 fusion.58
  336.9 47.8 %reduce-scatter.11.cloned.1.call-done = f32[128,1152]{1,0:T(8,128)} async-done(((f32[512,1152]{1,0:T(8,128)}), f32[128,1152]{1,0:T(8,128)}) %reduce-scatter.11.cloned.1.call-update) | async-done | bytes 589840 | tf_op jit(solution)/shard_map/reduce_scatter | solution.py:222
  385.9 2.1 fusion.20
  388.0 2.5 multiply_convert_fusion.4
  390.8 29.5 %all-gather.17.cloned.1.call-done = bf16[512,1152]{1,0:T(8,128)(2,1)} async-done(((bf16[128,1152]{1,0:T(8,128)(2,1)}), bf16[512,1152]{1,0:T(8,128)(2,1)}) %all-gather.17.cloned.1.call-update) | async-done | bytes 1179664 | tf_op jit(solution)/shard_map/all_gather | solution.py:228
  420.3 9.5 %multiply_convert_fusion = (bf16[512,1728]{0,1:T(8,128)(2,1)S(1)}, bf16[512,1728]{0,1:T(8,128)(2,1)S(1)}) fusion(f32[512,1728]{0,1:T(8,128)} %fusion.57, f32[512,1728]{0,1:T(8,128)} %get-tuple-element.76, bf16[512,1152]{1,0:T(8,128)(2,1)} %all-gather.17.cloned.1.call-done, bf16[1728,1152]{1,0:T(8,128)(2,1)} %all-gather.15.cloned.1.call-done), kind=kOutput, calls=%fused_computation.15 | convolution fusion | flops 2058780672 | bytes 15777792 | tf_op jit(solution)/shard_map/dot_general | solution.py:91
  429.8 2.7 fusion.59
  433.2 4.1 convolution_add_fusion
  437.7 4.4 convolution_convert_fusion
  442.1 2.5 convolution_convert_fusion.1
  444.6 2.5 convolution_convert_fusion.2
  447.1 5.0 pad_maximum_fusion
  452.2 3.5 fusion.13
  456.2 28.2 %reduce-scatter.13.cloned.1.call-done = f32[128,1152]{1,0:T(8,128)} async-done(((f32[512,1152]{1,0:T(8,128)}), f32[128,1152]{1,0:T(8,128)}) %reduce-scatter.13.cloned.1.call-update) | async-done | bytes 589840 | tf_op jit(solution)/shard_map/reduce_scatter | solution.py:239
  484.4 2.2 multiply_reduce_fusion
  486.6 2.8 multiply_reduce_fusion.1
  492.7 1.9 copy.123
  494.6 1.8 copy.125
  497.8 3.5 convolution_bitcast_fusion
  501.2 2.7 fusion.14
  512.4 2.9 fusion.60
  518.2 4.6 collective-permute-done.10
  525.6 1.8 multiply_reduce_fusion.14
  535.3 2.2 multiply_convert_fusion.7
  537.5 1.8 copy.126
  539.3 5.2 fusion.31
  544.5 104.5 %fusion = f32[40,1536]{1,0:T(8,128)} fusion(f32[1152,1536]{1,0:T(8,128)} %fusion.31), kind=kCustom, calls=%all-reduce-scatter | all-reduce-scatter fusion | flops 1966081 | bytes 7323648
  650.5 3.2 collective-permute-start.15
  653.7 7.3 collective-permute-start.14
  661.0 3.0 collective-permute-start.13
  664.0 1.9 collective-permute-start.16
  665.9 3.3 multiply_reduce_fusion.2
  669.3 39.8 %all-reduce.5 = (f32[4,1152]{1,0:T(4,128)S(1)}, f32[2,256]{1,0:T(2,128)S(1)}) all-reduce(f32[4,1152]{1,0:T(4,128)S(1)} %pad_maximum_fusion.12, f32[2,256]{1,0:T(2,128)S(1)} %pad_maximum_fusion.13), channel_id=7, replica_groups=mesh['seq'=4,'dp'=8] {'seq','dp'}, use_global_device_ids=true, to_apply=%region_26.27.clone | all-reduce | flops 5120 | bytes 40960
  709.7 2.4 add_bitcast_fusion
  712.7 4.1 concatenate.70
  717.6 3.0 fusion.55
  720.6 5.1 reduce-scatter.15.cloned.1.call-done
  (240 shorter events, 60.0 us)
Async XLA Ops:
  7.2 177.4 %all-gather.7.cloned.1.call-start = ((), (), s32[]{:S(2)}) async-start(), calls=%async_computation.4 | async-start | bytes 2433024 | tf_op jit(solution)/shard_map/all_gather | solution.py:161
  7.2 1.7 collective-permute-start
  9.9 9.2 %collective-permute-start.1 = (bf16[2,36,1536]{2,1,0:T(8,128)(2,1)S(1)}, bf16[2,36,1536]{2,1,0:T(8,128)(2,1)S(1)}, u32[]{:S(2)}, u32[]{:S(2)}) collective-permute-start(bf16[2,36,1536]{2,1,0:T(8,128)(2,1)S(1)} %pad_maximum_fusion.7), channel_id=1, source_target_pairs={{0,2},{1,3},{2,0},{3,1},{4,6},{5,7},{6,4},{7,5},{8,10},{9,11},{10,... | collective-permute-start | bytes 663560 | tf_op jit(solution)/shard_map/ppermute | solution.py:31
  19.2 12.8 %collective-permute-start.2 = (bf16[4,36,1536]{2,1,0:T(8,128)(2,1)S(1)}, bf16[4,36,1536]{2,1,0:T(8,128)(2,1)S(1)}, u32[]{:S(2)}, u32[]{:S(2)}) collective-permute-start(bf16[4,36,1536]{2,1,0:T(8,128)(2,1)S(1)} %pad_maximum_fusion.5), channel_id=1, source_target_pairs={{0,4},{1,5},{2,6},{3,7},{4,0},{5,1},{6,2},{7,3},{8,12},{9,13},{10,... | collective-permute-start | bytes 1327112 | tf_op jit(solution)/shard_map/ppermute | solution.py:31
  32.4 20.4 %collective-permute-start.3 = (bf16[8,36,1536]{2,0,1:T(8,128)(2,1)S(1)}, bf16[8,36,1536]{2,0,1:T(8,128)(2,1)}, u32[]{:S(2)}, u32[]{:S(2)}) collective-permute-start(bf16[8,36,1536]{2,0,1:T(8,128)(2,1)S(1)} %copy.114), channel_id=1, source_target_pairs={{0,8},{1,9},{2,10},{3,11},{4,12},{5,13},{6,14},{7,15},{8,0},{9,1},... | collective-permute-start | bytes 2654216 | tf_op jit(solution)/shard_map/ppermute | solution.py:31
  54.8 4.1 copy-start.57
  54.9 4.5 copy-start
  56.6 82.3 %collective-permute-start.4 = (bf16[16,36,1536]{2,0,1:T(8,128)(2,1)}, bf16[16,36,1536]{2,0,1:T(8,128)(2,1)}, u32[]{:S(2)}, u32[]{:S(2)}) collective-permute-start(bf16[16,36,1536]{2,0,1:T(8,128)(2,1)} %copy.117), channel_id=1, source_target_pairs={{0,16},{1,17},{2,18},{3,19},{4,20},{5,21},{6,22},{7,23},{8,24},{9,... | collective-permute-start | bytes 5308424 | tf_op jit(solution)/shard_map/ppermute | solution.py:31
  58.9 159.4 %all-gather.9.cloned.1.call-start = ((), (), s32[]{:S(2)}) async-start(), calls=%async_computation.5 | async-start | bytes 1474560 | tf_op jit(solution)/shard_map/all_gather | solution.py:213
  59.5 89.2 %copy-start.45 = (f32[128]{0:T(128)}, f32[128]{0:T(128)S(1)}, u32[]{:S(2)}) copy-start(f32[128]{0:T(128)S(1)} %add_rsqrt_fusion.5) | copy-start | bytes 1540
  144.7 4.0 copy-start.31
  150.6 14.5 %copy-start.15 = (f32[128,1536]{1,0:T(8,128)}, f32[128,1536]{1,0:T(8,128)S(1)}, u32[]{:S(2)}) copy-start(f32[128,1536]{1,0:T(8,128)S(1)} %fusion.29) | copy-start | bytes 2359300
  150.6 20.3 %copy-start.43 = (f32[256]{0:T(256)S(1)}, f32[256]{0:T(256)}, u32[]{:S(2)}) copy-start(f32[256]{0:T(256)} %param.23) | copy-start | bytes 3076
  150.8 4.6 copy-start.47
  154.1 19.3 %collective-permute-start.5 = (bf16[128,512]{1,0:T(8,128)(2,1)}, bf16[128,512]{1,0:T(8,128)(2,1)}, u32[]{:S(2)}, u32[]{:S(2)}) collective-permute-start(bf16[128,512]{1,0:T(8,128)(2,1)} %pad_maximum_fusion.11), channel_id=1, source_target_pairs={} | collective-permute-start | bytes 393224 | tf_op jit(solution)/shard_map/ppermute | solution.py:43
  155.4 19.0 %collective-permute-start.6 = (bf16[128,512]{1,0:T(8,128)(2,1)}, bf16[128,512]{1,0:T(8,128)(2,1)}, u32[]{:S(2)}, u32[]{:S(2)}) collective-permute-start(bf16[128,512]{1,0:T(8,128)(2,1)} %pad_maximum_fusion.11), channel_id=1, source_target_pairs={{0,24},{1,25},{2,26},{3,27},{4,28},{5,29},{6,30},{7,31}} | collective-permute-start | bytes 393224 | tf_op jit(solution)/shard_map/ppermute | solution.py:43
  160.7 14.6 %collective-permute-start.7 = (bf16[128,512]{1,0:T(8,128)(2,1)}, bf16[128,512]{1,0:T(8,128)(2,1)}, u32[]{:S(2)}, u32[]{:S(2)}) collective-permute-start(bf16[128,512]{1,0:T(8,128)(2,1)} %pad_maximum_fusion.11), channel_id=1, source_target_pairs={{0,16},{8,24},{1,17},{9,25},{2,18},{10,26},{3,19},{11,27},{4,20},{... | collective-permute-start | bytes 393224 | tf_op jit(solution)/shard_map/ppermute | solution.py:43
  162.7 13.6 %collective-permute-start.8 = (bf16[128,512]{1,0:T(8,128)(2,1)}, bf16[128,512]{1,0:T(8,128)(2,1)}, u32[]{:S(2)}, u32[]{:S(2)}) collective-permute-start(bf16[128,512]{1,0:T(8,128)(2,1)} %pad_maximum_fusion.11), channel_id=1, source_target_pairs={{0,8},{8,16},{16,24},{1,9},{9,17},{17,25},{2,10},{10,18},{18,26},{... | collective-permute-start | bytes 393224 | tf_op jit(solution)/shard_map/ppermute | solution.py:43
  170.9 6.3 copy-start.34
  170.9 6.3 copy-start.28
  170.9 6.3 copy-start.30
  184.5 4.3 copy-start.32
  189.7 65.5 %all-gather.11.cloned.1.call-start = ((), (), s32[]{:S(2)}) async-start(), calls=%async_computation.6 | async-start | bytes 4478976 | tf_op jit(solution)/shard_map/all_gather | solution.py:217
  190.4 102.2 %all-gather.13.cloned.1.call-start = ((), (), s32[]{:S(2)}) async-start(), calls=%async_computation.7 | async-start | bytes 4478976 | tf_op jit(solution)/shard_map/all_gather | solution.py:218
  191.0 139.1 %all-gather.15.cloned.1.call-start = ((), (), s32[]{:S(2)}) async-start(), calls=%async_computation.8 | async-start | bytes 4478976 | tf_op jit(solution)/shard_map/all_gather | solution.py:219
  191.6 193.1 %reduce-scatter.11.cloned.1.call-start = ((), (), s32[]{:S(2)}) async-start(), calls=%async_computation.9 | async-start | bytes 2949120 | tf_op jit(solution)/shard_map/reduce_scatter | solution.py:222
  336.8 83.5 %all-gather.17.cloned.1.call-start = ((), (), s32[]{:S(2)}) async-start(), calls=%async_computation.10 | async-start | bytes 1474560 | tf_op jit(solution)/shard_map/all_gather | solution.py:228
  390.5 93.9 %reduce-scatter.13.cloned.1.call-start = ((), (), s32[]{:S(2)}) async-start(), calls=%async_computation.11 | async-start | bytes 2949120 | tf_op jit(solution)/shard_map/reduce_scatter | solution.py:239
  420.3 9.5 %copy-start.55 = (bf16[1728,1152]{1,0:T(8,128)(2,1)S(1)}, bf16[1728,1152]{1,0:T(8,128)(2,1)}, u32[]{:S(2)}) copy-start(bf16[1728,1152]{1,0:T(8,128)(2,1)} %all-gather.11.cloned.1.call-done) | copy-start | bytes 11943940
  437.4 280.2 %reduce-scatter.17.cloned.1.call-start = ((), (), s32[]{:S(2)}) async-start(), calls=%async_computation.13 | async-start | bytes 13436928
  437.7 4.4 copy-start.13
  437.7 4.4 copy-start.56
  452.1 273.6 %reduce-scatter.15.cloned.1.call-start = ((), (), s32[]{:S(2)}) async-start(), calls=%async_computation.12 | async-start | bytes 4866048 | tf_op jit(solution)/shard_map/reduce_scatter | solution.py:307
  484.4 5.8 copy-start.7
  484.4 5.8 copy-start.33
  484.4 5.8 copy-start.50
  486.6 4.5 copy-start.8
  501.2 4.8 copy-start.18
  504.8 7.6 %copy-start.17 = (bf16[128,1152]{1,0:T(8,128)(2,1)S(1)}, bf16[128,1152]{1,0:T(8,128)(2,1)}, u32[]{:S(2)}) copy-start(bf16[128,1152]{1,0:T(8,128)(2,1)} %copy-done.16) | copy-start | bytes 884740
  504.8 7.6 %copy-start.19 = (bf16[128,4,256]{0,2,1:T(8,128)(2,1)S(1)}, bf16[128,4,256]{0,2,1:T(8,128)(2,1)}, u32[]{:S(2)}) copy-start(bf16[128,4,256]{0,2,1:T(8,128)(2,1)} %copy.122) | copy-start | bytes 786436
  506.9 10.4 %collective-permute-start.12 = (bf16[128,512]{1,0:T(8,128)(2,1)}, bf16[128,512]{1,0:T(8,128)(2,1)}, u32[]{:S(2)}, u32[]{:S(2)}) collective-permute-start(bf16[128,512]{1,0:T(8,128)(2,1)} %get-tuple-element.44), channel_id=1, source_target_pairs={} | collective-permute-start | bytes 393224 | tf_op jit(solution)/shard_map/ppermute | solution.py:43
  508.2 10.0 %collective-permute-start.11 = (bf16[128,512]{1,0:T(8,128)(2,1)}, bf16[128,512]{1,0:T(8,128)(2,1)}, u32[]{:S(2)}, u32[]{:S(2)}) collective-permute-start(bf16[128,512]{1,0:T(8,128)(2,1)} %get-tuple-element.45), channel_id=1, source_target_pairs={{24,0},{25,1},{26,2},{27,3},{28,4},{29,5},{30,6},{31,7}} | collective-permute-start | bytes 393224 | tf_op jit(solution)/shard_map/ppermute | solution.py:43
  509.4 13.3 %collective-permute-start.10 = (bf16[128,512]{1,0:T(8,128)(2,1)}, bf16[128,512]{1,0:T(8,128)(2,1)}, u32[]{:S(2)}, u32[]{:S(2)}) collective-permute-start(bf16[128,512]{1,0:T(8,128)(2,1)} %get-tuple-element.46), channel_id=1, source_target_pairs={{16,0},{24,8},{17,1},{25,9},{18,2},{26,10},{19,3},{27,11},{20,4},{... | collective-permute-start | bytes 393224 | tf_op jit(solution)/shard_map/ppermute | solution.py:43
  510.7 4.5 copy-start.37
  510.8 12.0 %collective-permute-start.9 = (bf16[128,512]{1,0:T(8,128)(2,1)}, bf16[128,512]{1,0:T(8,128)(2,1)}, u32[]{:S(2)}, u32[]{:S(2)}) collective-permute-start(bf16[128,512]{1,0:T(8,128)(2,1)} %get-tuple-element.43), channel_id=1, source_target_pairs={{8,0},{16,8},{24,16},{9,1},{17,9},{25,17},{10,2},{18,10},{26,18},{... | collective-permute-start | bytes 393224 | tf_op jit(solution)/shard_map/ppermute | solution.py:43
  517.2 8.3 %copy-start.26 = (f32[128,128]{1,0:T(8,128)S(1)}, f32[128,128]{1,0:T(8,128)}, u32[]{:S(2)}) copy-start(f32[128,128]{1,0:T(8,128)} %copy-done.25) | copy-start | bytes 196612
  517.2 8.3 %copy-start.42 = (f32[256]{0:T(256)S(1)}, f32[256]{0:T(256)}, u32[]{:S(2)}) copy-start(f32[256]{0:T(256)} %param.24) | copy-start | bytes 3076
  517.2 8.3 %copy-start.48 = (f32[128]{0:T(128)S(1)}, f32[128]{0:T(128)}, u32[]{:S(2)}) copy-start(f32[128]{0:T(128)} %copy-done.47) | copy-start | bytes 1540
  517.2 10.1 %copy-start.10 = (bf16[128,4,640]{2,0,1:T(8,128)(2,1)S(1)}, bf16[128,4,640]{2,0,1:T(8,128)(2,1)}, u32[]{:S(2)}) copy-start(bf16[128,4,640]{2,0,1:T(8,128)(2,1)} %copy-done.9) | copy-start | bytes 1966084
  517.3 10.1 %copy-start.23 = (bf16[640,512]{1,0:T(8,128)(2,1)S(1)}, bf16[640,512]{1,0:T(8,128)(2,1)}, u32[]{:S(2)}) copy-start(bf16[640,512]{1,0:T(8,128)(2,1)} %copy-done.22) | copy-start | bytes 1966084
  524.0 5.4 copy-start.3
  524.0 5.4 copy-start.35
  524.0 5.4 copy-start.44
  544.5 121.4 %copy-start.46 = (f32[128]{0:T(128)S(1)}, f32[128]{0:T(128)}, u32[]{:S(2)}) copy-start(f32[128]{0:T(128)} %copy-done.45) | copy-start | bytes 1540
  650.4 18.8 %copy-start.52 = (f32[256]{0:T(256)S(1)}, f32[256]{0:T(256)}, u32[]{:S(2)}) copy-start(f32[256]{0:T(256)} %get-tuple-element.21) | copy-start | bytes 3076
  650.4 18.8 %copy-start.53 = (f32[256]{0:T(256)S(1)}, f32[256]{0:T(256)}, u32[]{:S(2)}) copy-start(f32[256]{0:T(256)} %get-tuple-element.23) | copy-start | bytes 3076
  650.4 18.8 %copy-start.38 = (f32[1,1152]{1,0:T(1,128)S(1)}, f32[1,1152]{1,0:T(1,128)}, u32[]{:S(2)}) copy-start(f32[1,1152]{1,0:T(1,128)} %stack.27) | copy-start | bytes 13828
  650.4 18.8 %copy-start.39 = (f32[1,1152]{1,0:T(1,128)S(1)}, f32[1,1152]{1,0:T(1,128)}, u32[]{:S(2)}) copy-start(f32[1,1152]{1,0:T(1,128)} %stack.26) | copy-start | bytes 13828
  650.4 18.8 %copy-start.40 = (f32[1,1152]{1,0:T(1,128)S(1)}, f32[1,1152]{1,0:T(1,128)}, u32[]{:S(2)}) copy-start(f32[1,1152]{1,0:T(1,128)} %stack.25) | copy-start | bytes 13828
  650.5 62.3 %collective-permute-start.15 = (f32[40,1536]{1,0:T(8,128)}, f32[40,1536]{1,0:T(8,128)}, u32[]{:S(2)}, u32[]{:S(2)}) collective-permute-start(f32[40,1536]{1,0:T(8,128)} %fusion), channel_id=1, source_target_pairs={{0,3},{1,4},{2,5},{3,6},{4,7},{5,8},{6,9},{7,10},{8,11},{9,12},{10... | collective-permute-start | bytes 737288
  653.7 59.0 %collective-permute-start.14 = (f32[40,1536]{1,0:T(8,128)}, f32[40,1536]{1,0:T(8,128)}, u32[]{:S(2)}, u32[]{:S(2)}) collective-permute-start(f32[40,1536]{1,0:T(8,128)} %fusion), channel_id=1, source_target_pairs={{0,2},{1,3},{2,4},{3,5},{4,6},{5,7},{6,8},{7,9},{8,10},{9,11},{10,... | collective-permute-start | bytes 737288
  661.0 51.7 %collective-permute-start.13 = (f32[40,1536]{1,0:T(8,128)}, f32[40,1536]{1,0:T(8,128)}, u32[]{:S(2)}, u32[]{:S(2)}) collective-permute-start(f32[40,1536]{1,0:T(8,128)} %fusion), channel_id=1, source_target_pairs={{0,1},{1,2},{2,3},{3,4},{4,5},{5,6},{6,7},{7,8},{8,9},{9,10},{10,1... | collective-permute-start | bytes 737288
  664.0 48.7 %collective-permute-start.16 = (f32[4,1536]{1,0:T(4,128)}, f32[4,1536]{1,0:T(4,128)}, u32[]{:S(2)}, u32[]{:S(2)}) collective-permute-start(f32[4,1536]{1,0:T(4,128)} %slice.146), channel_id=1, source_target_pairs={{0,4},{1,5},{2,6},{3,7},{4,8},{5,9},{6,10},{7,11},{8,12},{9,13},{1... | collective-permute-start | bytes 73736
  669.2 43.5 %copy-start.24 = (f32[40,1536]{1,0:T(8,128)S(1)}, f32[40,1536]{1,0:T(8,128)}, u32[]{:S(2)}) copy-start(f32[40,1536]{1,0:T(8,128)} %fusion) | copy-start | bytes 737284
  (23 other events, 42.6 us)
Sparse Core Ops, SparseCore 0:
  59.0 101.6 all-gather.6
  189.8 28.4 all-gather.8
  220.2 34.9 all-gather.10
  256.9 35.6 all-gather.12
  294.4 35.6 all-gather.14
  336.9 47.6 reduce-scatter.10
  390.7 29.6 all-gather.16
  437.5 46.9 reduce-scatter.12
  488.0 104.7 reduce-scatter.16
  598.7 126.9 reduce-scatter.14
